TPU v7x, 32 devices: a whole 2x2x4 slice. The times are simulated.
32 devices in a mesh: gx: 8 (over y, x, core), yz: 4 (over z).
Axes of the slice: x: 2, y: 2, z: 4, core: 2. Of those that a mesh axis runs over, the one named last changes fastest.
Arguments:
- residual: float32 [96, 8, 64, 128], P('gx', 'yz'), may hold values from -0.3 to 0.3
- inverses: float32 [96, 8, 64, 64], P('gx', 'yz'), may hold values from -0.25 to 1
- upwind: float32 [8, 64, 64], replicated, may hold values from -0.25 to 1
- downwind: float32 [8, 64, 64], replicated, may hold values from -0.25 to 1
- flux_y: float32 [8, 64, 64], replicated, may hold values from -0.75 to 0.75
- kinds: int32 [8], P('yz'), may hold values from 0 to 7
- volume_category: int32 [96, 8, 128], P('gx', 'yz'), may hold values from 0 to 2, as said below
Outputs:
- adjoint: float32 [96, 8, 64, 128], P('gx', 'yz')
Inputs may be any that keep to these rules, and one draw needn't show every extreme that they name: `volume_category`: 0 marks a fluid cell, 1 a wall cell, 2 an inflow cell.
All inputs are finite; a program needn't handle non-finite values.
Results may differ from a plain program's by a relative error of at most 0.00026.
Values sent between devices are 32-bit elements; how exact they have to be, the bound alone decides.
A program may use at most 64 MiB of HBM per device.

v0:
```python
import jax
import jax.numpy as jnp
from jax import lax
from jax.sharding import PartitionSpec as P

HIGHEST = lax.Precision.HIGHEST


def carried_in(part, axis, combine, identity, reverse):
    count = lax.axis_size(axis)
    place = lax.axis_index(axis)
    ahead = count - 1 - place if reverse else place
    gathered = jax.tree.map(lambda a: lax.all_gather(a, axis), part)
    state = jax.tree.map(lambda a, e: jnp.zeros_like(a) + jnp.asarray(e, a.dtype), part, identity)

    def one(step, state):
        source = count - 1 - step if reverse else step
        return combine(
            state, jax.tree.map(lambda a: lax.dynamic_index_in_dim(a, source, 0, False), gathered)
        )

    return lax.fori_loop(0, ahead, one, state)


def extended(block, sides, width):
    for axis, dim in sides:
        count = lax.axis_size(axis)
        forward = [(i, i + 1) for i in range(count - 1)]
        backward = [(target, source) for source, target in forward]
        low = lax.ppermute(
            lax.slice_in_dim(block, block.shape[dim] - width, None, axis=dim), axis, forward
        )
        high = lax.ppermute(lax.slice_in_dim(block, 0, width, axis=dim), axis, backward)
        block = jnp.concatenate([low, block, high], axis=dim)
    return block


def apply_transposed(matrices, vectors):
    return jnp.einsum("gab,gaz->gbz", matrices, vectors, precision=HIGHEST)


def select_rows(kinds, table):
    kind_count = table.shape[0]
    one_hot = (kinds[:, None] == jnp.arange(kind_count, dtype=jnp.int32)[None, :]).astype(
        jnp.float32
    )
    flat = jnp.dot(
        one_hot,
        table.reshape(kind_count, -1),
        precision=HIGHEST,
        preferred_element_type=jnp.float32,
    )
    return flat.reshape(kinds.shape[0], table.shape[1], table.shape[2])


def source_weight(volume_category):
    fluid = (volume_category == 0).astype(jnp.float32)
    inflow = (volume_category == 2).astype(jnp.float32)
    return (fluid + 0.5 * inflow)[:, :, None, :]


def y_derivative(padded):
    return (8.0 * (padded[:, 3:-1] - padded[:, 1:-3]) - (padded[:, 4:] - padded[:, :-4])) / 12.0


def combine_maps(earlier, later):
    early_map, early_offset = earlier
    late_map, late_offset = later
    joined = jnp.einsum("gab,gbc->gac", early_map, late_map, precision=HIGHEST)
    return (joined, apply_transposed(late_map, early_offset) + late_offset)


def compose_steps(steps, identity, reverse):

    def multiply(accum, step_block):
        return (jnp.einsum("gab,gbc->gac", accum, step_block, precision=HIGHEST), None)

    composed, unused = lax.scan(multiply, identity, steps, reverse=reverse)
    return composed


def line_inflow(mapping, offsets, identity, zero_lines, reverse):
    prefix = carried_in((mapping, offsets), "gx", combine_maps, (identity, zero_lines), reverse)
    return prefix[1]


def per_device(residual, inverses, upwind, downwind, flux_y, kinds, volume_category):
    up_rows = select_rows(kinds, upwind)
    lower_neighbors = select_rows(kinds, downwind)
    flux_rows = select_rows(kinds, flux_y)
    padded = extended(residual, (("yz", 1),), 2)
    derivative = y_derivative(padded)
    flux = jnp.einsum("yab,xyaz->xybz", flux_rows, derivative, precision=HIGHEST)
    forcing = source_weight(volume_category) * (residual + flux)
    groups = residual.shape[1]
    variables = residual.shape[2]
    line_count = residual.shape[3]
    zero_lines = jnp.zeros((groups, variables, line_count), jnp.float32)
    identity = jnp.broadcast_to(
        jnp.eye(variables, dtype=jnp.float32), (groups, variables, variables)
    )

    def forward_step(carried, cell_data):
        forcing_cell, inverse_cell = cell_data
        eliminated = forcing_cell - apply_transposed(up_rows, carried)
        return (apply_transposed(inverse_cell, eliminated), eliminated)

    def forward_pass(entering):
        return lax.scan(forward_step, entering, (forcing, inverses))

    leaving_zero, unused_forward = forward_pass(zero_lines)
    forward_steps = -jnp.einsum("gab,xgbc->xgac", up_rows, inverses, precision=HIGHEST)
    forward_map = compose_steps(forward_steps, identity, False)
    entering = line_inflow(forward_map, leaving_zero, identity, zero_lines, False)
    leaving_final, eliminated = forward_pass(entering)

    def backward_step(carried, cell_data):
        eliminated_cell, inverse_cell = cell_data
        updated = apply_transposed(
            inverse_cell, eliminated_cell - apply_transposed(lower_neighbors, carried)
        )
        return (updated, updated)

    def backward_pass(entering_back):
        return lax.scan(backward_step, entering_back, (eliminated, inverses), reverse=True)

    first_zero, unused_backward = backward_pass(zero_lines)
    backward_steps = -jnp.einsum("gab,xgbc->xgac", lower_neighbors, inverses, precision=HIGHEST)
    backward_map = compose_steps(backward_steps, identity, True)
    entering_back = line_inflow(backward_map, first_zero, identity, zero_lines, True)
    first_final, adjoint = backward_pass(entering_back)
    wet_cells = (volume_category != 1).astype(jnp.float32)[:, :, None, :]
    return adjoint * wet_cells


def solution(mesh):
    in_specs = (
        P("gx", "yz", None, None),
        P("gx", "yz", None, None),
        P(),
        P(),
        P(),
        P("yz"),
        P("gx", "yz", None),
    )
    out_specs = P("gx", "yz", None, None)
    return jax.shard_map(
        per_device, mesh=mesh, in_specs=in_specs, out_specs=out_specs, check_vma=False
    )
```

profile of v0, /device:TPU:1, one launch (start us, length us, event | category | flops | bytes accessed | tf_op | source)
XLA Modules:
  0.0 90.0 jit_solution(17059266296134466561)
XLA Ops:
  0.0 1.3 %collective-permute-start = (f32[12,2,64,128]{3,2,1,0:T(8,128)}, f32[12,2,64,128]{3,2,1,0:T(8,128)}, u32[]{:S(2)}, u32[]{:S(2)}) collective-permute-start(f32[12,2,64,128]{3,2,1,0:T(8,128)} %param.23), channel_id=1, source_target_pairs={{1,0},{2,1},{3,2},{5,4},{6,5},{7,6},{9,8},{10,9},{11,10},{13,12},{... | collective-permute-start | bytes 2359304 | tf_op jit(solution)/shard_map/ppermute | solution.py:33
  1.3 5.6 %collective-permute-start.1 = (f32[12,2,64,128]{3,2,1,0:T(8,128)}, f32[12,2,64,128]{3,2,1,0:T(8,128)}, u32[]{:S(2)}, u32[]{:S(2)}) collective-permute-start(f32[12,2,64,128]{3,2,1,0:T(8,128)} %param.23), channel_id=1, source_target_pairs={{0,1},{1,2},{2,3},{4,5},{5,6},{6,7},{8,9},{9,10},{10,11},{12,13},{... | collective-permute-start | bytes 2359304 | tf_op jit(solution)/shard_map/ppermute | solution.py:30
  6.9 1.1 %reshape.19 = f32[8,4096]{1,0:T(8,128)S(1)} reshape(f32[8,64,64]{2,1,0:T(8,128)} %param.25) | data formatting | bytes 262144 | tf_op jit(solution)/shard_map/reshape | solution.py:49
  8.0 0.8 copy-done.2
  9.1 0.6 copy-done.5
  9.7 0.4 fusion.40
  10.1 0.4 fusion.42
  10.5 0.8 fusion.29
  11.3 0.8 fusion.30
  12.2 4.0 %while.102 = (s32[]{:T(128)}, f32[2,64,64]{1,2,0:T(8,128)S(1)}, f32[12,2,64,64]{3,2,0,1:T(8,128)S(1)}, s32[]{:T(128)}, s32[]{:T(128)}) while((s32[]{:T(128)}, f32[2,64,64]{1,2,0:T(8,128)S(1)}, f32[12,2,64,64]{3,2,0,1:T(8,128)S(1)}, s32[]{:T(128)}, s32[]{:T(128)}) %tuple.205), condition=%wide.region_1.2_spmd, body=%wide.region_0.1_spmd.sunk | while | flops 6291459 | bytes 229453 | solution.py:78
  16.2 4.0 %while.103 = (s32[]{:T(128)}, f32[2,64,64]{1,2,0:T(8,128)S(1)}, f32[12,2,64,64]{3,2,0,1:T(8,128)S(1)}, s32[]{:T(128)}) while((s32[]{:T(128)}, f32[2,64,64]{1,2,0:T(8,128)S(1)}, f32[12,2,64,64]{3,2,0,1:T(8,128)S(1)}, s32[]{:T(128)}) %tuple.208), condition=%wide.region_3.4_spmd, body=%wide.region_2.3_spmd.sunk | while | flops 6291458 | bytes 229433 | solution.py:78
  20.6 0.8 copy-done.3
  21.6 0.6 copy-done.4
  22.4 11.2 %all-gather.1 = f32[16,64,64]{2,1,0:T(8,128)S(1)} all-gather(f32[2,64,64]{2,1,0:T(8,128)S(1)} %copy.91), channel_id=3, replica_groups=mesh['gx'=8,'yz'=4] {'gx'}, dimensions={0}, use_global_device_ids=true | all-gather | bytes 294912 | tf_op jit(solution)/shard_map/all_gather | solution.py:13
  33.6 9.8 %all-gather = f32[16,64,64]{2,1,0:T(8,128)S(1)} all-gather(f32[2,64,64]{2,1,0:T(8,128)S(1)} %copy.86), channel_id=2, replica_groups=mesh['gx'=8,'yz'=4] {'gx'}, dimensions={0}, use_global_device_ids=true | all-gather | bytes 294912 | tf_op jit(solution)/shard_map/all_gather | solution.py:13
  43.4 0.4 convolution_bitcast_fusion.3
  43.9 2.6 %fusion.31 = f32[12,2,64,128]{3,2,0,1:T(8,128)S(1)} fusion(f32[12,2,64,128]{3,2,1,0:T(8,128)S(1)} %copy-done.1, f32[12,2,128]{2,0,1:T(8,128)S(1)} %copy.92, f32[2,64,64,1]{2,0,1,3:T(2,128)S(1)} %convolution_bitcast_fusion.3, f32[12,2,64,128]{3,2,1,0:T(8,128)} %collective-permute-done.1, f32[12,2,64,128]{3,2,1,0:T(8,128)} %collective-permute-done), kind=kOutput, calls=%fused_computation.44 | convolution fusion | flops 152764416 | bytes 3190784 | tf_op jit(solution)/shard_map/yab,xyaz->xybz/dot_general | solution.py:93
  46.6 5.0 %while.104 = (s32[]{:T(128)}, f32[2,64,128]{2,1,0:T(8,128)S(1)}, f32[12,2,64,64]{2,3,1,0:T(8,128)S(1)}, f32[12,2,64,128]{3,2,1,0:T(8,128)S(1)}, f32[2,64,64]{1,2,0:T(8,128)S(1)}, /*index=5*/s32[]{:T(128)}) while((s32[]{:T(128)}, f32[2,64,128]{2,1,0:T(8,128)S(1)}, f32[12,2,64,64]{2,3,1,0:T(8,128)S(1)}, f32[12,2,64,128]{3,2,1,0:T(8,128)S(1)}, ...), condition=%wide.region_5.6_spmd, body=%wide.region_4.5_spmd.sunk | while | flops 25182208 | bytes 426061 | solution.py:109
  51.6 8.9 %all-gather.2 = f32[16,64,128]{2,1,0:T(8,128)S(1)} all-gather(f32[2,64,128]{2,1,0:T(8,128)S(1)} %get-tuple-element.501), channel_id=4, replica_groups=mesh['gx'=8,'yz'=4] {'gx'}, dimensions={0}, use_global_device_ids=true | all-gather | bytes 589824 | tf_op jit(solution)/shard_map/all_gather | solution.py:13
  60.5 0.3 while.105
  60.5 0.3 convolution_add_fusion.4
  60.9 5.0 %while.106 = (s32[]{:T(128)}, f32[2,64,128]{2,1,0:T(8,128)S(1)}, f32[12,2,64,128]{3,2,1,0:T(8,128)S(1)}, f32[12,2,64,64]{2,3,1,0:T(8,128)S(1)}, f32[12,2,64,128]...) while((s32[]{:T(128)}, f32[2,64,128]{2,1,0:T(8,128)S(1)}, f32[12,2,64,128]{3,2,1,0:T(8,128)S(1)}, ...), condition=%wide.region_9.10_spmd, body=%wide.region_8.9_spmd.sunk | while | flops 25182208 | bytes 524373 | solution.py:109
  65.9 5.0 %while.107 = (s32[]{:T(128)}, f32[2,64,128]{2,1,0:T(8,128)S(1)}, f32[12,2,64,64]{2,3,1,0:T(8,128)S(1)}, f32[12,2,64,128]{3,2,1,0:T(8,128)S(1)}, f32[2,64,64]{1,2,0:T(8,128)S(1)}, /*index=5*/s32[]{:T(128)}, s32[]{:T(128)}) while((s32[]{:T(128)}, f32[2,64,128]{2,1,0:T(8,128)S(1)}, f32[12,2,64,64]{2,3,1,0:T(8,128)S(1)}, ...), condition=%wide.region_11.12_spmd, body=%wide.region_10.11_spmd.sunk | while | flops 25182212 | bytes 426081 | solution.py:125
  70.9 10.9 %all-gather.3 = f32[16,64,128]{2,1,0:T(8,128)S(1)} all-gather(f32[2,64,128]{2,1,0:T(8,128)S(1)} %get-tuple-element.504), channel_id=5, replica_groups=mesh['gx'=8,'yz'=4] {'gx'}, dimensions={0}, use_global_device_ids=true | all-gather | bytes 589824 | tf_op jit(solution)/shard_map/all_gather | solution.py:13
  81.9 2.1 %while.108 = (s32[]{:T(128)}, f32[2,64,128]{2,1,0:T(8,128)S(1)}, s32[]{:T(128)}, f32[8,2,64,64]{3,2,1,0:T(8,128)S(1)}, f32[8,2,64,128]{3,2,1,0:T(8,128)S(1)}, /*index=5*/s32[]{:T(128)}, s32[]{:T(128)}, s32[]{:T(128)}, s32[]{:T(128)}) while((s32[]{:T(128)}, f32[2,64,128]{2,1,0:T(8,128)S(1)}, s32[]{:T(128)}, f32[8,2,64,64]{3,2,1,0:T(8,128)S(1)}, ...), condition=%wide.region_13.14_spmd, body=%wide.region_12.13_spmd.sunk | while | flops 12599302 | bytes 394379 | solution.py:22
  81.9 0.3 convolution_add_fusion.5
  82.3 0.3 convolution_add_fusion.5
  82.6 0.3 convolution_add_fusion.5
  83.0 0.3 convolution_add_fusion.5
  83.3 0.3 convolution_add_fusion.5
  84.0 5.0 %while.109 = (s32[]{:T(128)}, f32[2,64,128]{2,1,0:T(8,128)S(1)}, f32[12,2,64,128]{3,2,1,0:T(8,128)S(1)}, f32[12,2,64,64]{2,3,1,0:T(8,128)S(1)}, f32[12,2,64,128]...) while((s32[]{:T(128)}, f32[2,64,128]{2,1,0:T(8,128)S(1)}, ...), condition=%wide.region_15.16_spmd, body=%wide.region_14.15_spmd.sunk | while | flops 25182212 | bytes 492645 | solution.py:125
  89.1 1.0 %broadcast_multiply_fusion = f32[12,2,64,128]{3,2,1,0:T(8,128)} fusion(f32[12,2,64,128]{3,2,1,0:T(8,128)S(1)} %get-tuple-element.506, f32[12,2,128]{2,1,0:T(2,128)S(1)} %compare_convert_fusion), kind=kLoop, calls=%fused_computation.55 | loop fusion | flops 196608 | bytes 1585152 | tf_op jit(solution)/shard_map/mul | solution.py:133
  (185 shorter events, 27.6 us)
Async XLA Ops:
  0.0 43.9 %collective-permute-start = (f32[12,2,64,128]{3,2,1,0:T(8,128)}, f32[12,2,64,128]{3,2,1,0:T(8,128)}, u32[]{:S(2)}, u32[]{:S(2)}) collective-permute-start(f32[12,2,64,128]{3,2,1,0:T(8,128)} %param.23), channel_id=1, source_target_pairs={{1,0},{2,1},{3,2},{5,4},{6,5},{7,6},{9,8},{10,9},{11,10},{13,12},{... | collective-permute-start | bytes 2359304 | tf_op jit(solution)/shard_map/ppermute | solution.py:33
  1.3 42.6 %collective-permute-start.1 = (f32[12,2,64,128]{3,2,1,0:T(8,128)}, f32[12,2,64,128]{3,2,1,0:T(8,128)}, u32[]{:S(2)}, u32[]{:S(2)}) collective-permute-start(f32[12,2,64,128]{3,2,1,0:T(8,128)} %param.23), channel_id=1, source_target_pairs={{0,1},{1,2},{2,3},{4,5},{5,6},{6,7},{8,9},{9,10},{10,11},{12,13},{... | collective-permute-start | bytes 2359304 | tf_op jit(solution)/shard_map/ppermute | solution.py:30
  7.9 1.0 %copy-start.2 = (f32[8,64,64]{2,1,0:T(8,128)S(1)}, f32[8,64,64]{2,1,0:T(8,128)}, u32[]{:S(2)}) copy-start(f32[8,64,64]{2,1,0:T(8,128)} %param.26) | copy-start | bytes 393220
  8.9 1.7 %copy-start = (f32[12,2,64,64]{3,2,1,0:T(8,128)S(1)}, f32[12,2,64,64]{3,2,1,0:T(8,128)}, u32[]{:S(2)}) copy-start(f32[12,2,64,64]{3,2,1,0:T(8,128)} %param.24) | copy-start | bytes 1179652
  9.0 0.7 copy-start.5
  20.4 1.0 %copy-start.3 = (f32[8,64,64]{2,1,0:T(8,128)S(1)}, f32[8,64,64]{2,1,0:T(8,128)}, u32[]{:S(2)}) copy-start(f32[8,64,64]{2,1,0:T(8,128)} %param.27) | copy-start | bytes 393220
  21.5 0.7 copy-start.4
  22.4 21.5 %copy-start.1 = (f32[12,2,64,128]{3,2,1,0:T(8,128)S(1)}, f32[12,2,64,128]{3,2,1,0:T(8,128)}, u32[]{:S(2)}) copy-start(f32[12,2,64,128]{3,2,1,0:T(8,128)} %param.23) | copy-start | bytes 2359300
where the time goes:
time: 90.9 us; the launch traced here: 90 us
  blocking collectives  40.8 us (45%)
  matrix products  33.2 us (37%)
  starting transfers between devices  6.84 us (8%)
  local copies, waits for them, and re-layouts  5.46 us (6%)
  loops' own time  2.41 us (3%)
  other arithmetic  0.98 us (1%)
    all_gather x4, blocking collectives, carried_in(): gathered = jax.tree.map(lambda a: lax.all_gather(a, axis), part)  40.8 us
    dot_general x103, matrix products, apply_transposed(): return jnp.einsum('gab,gaz->gbz', matrices, vectors, precision=HIGHEST)  20.6 us
    dot_general x24, matrix products, multiply(): jnp.einsum('gab,gbc->gac', accum, step_block, precision=HIGHEST)  7.11 us
    ppermute x1, starting transfers between devices, extended(): lax.ppermute(lax.slice_in_dim(block, block.shape[dim] - width, None, axis...  5.56 us
    unnamed x12, local copies, waits for them, and re-layouts  2.82 us
    dot_general x1, matrix products, per_device(): jnp.einsum('yab,xyaz->xybz', flux_rows, derivative, precision=HIGHEST)  2.62 us
  transfers between devices with their start and end apart: 2, of which 0 were waited for; matrix products, arithmetic and copies ran while one was open for 14% of the time, Pallas kernels for 0%

commit v1 on v0

v1 whole, which is shorter than its diff:
```python
import functools

import jax
import jax.numpy as jnp
from jax import lax
from jax.experimental import pallas as pl
from jax.experimental.pallas import tpu as pltpu
from jax.sharding import PartitionSpec as P

MESH = pl.DeviceIdType.MESH
F32 = jnp.float32
BF16 = jnp.bfloat16


def split(a):
    high = a.astype(BF16)
    return high, (a - high.astype(F32)).astype(BF16)


def mul(a, b):
    ah, al = a
    bh, bl = b
    d = functools.partial(jnp.dot, preferred_element_type=F32)
    return d(ah, bh) + (d(ah, bl) + d(al, bh))


def kernel(
    n_gx, n_yz, chunk, kinds, res, inv, up, down, flux, cat, out,
    snd, low, high, table, vt, ft, bt, hom, resp, cs, gmap, gvec, cin, into,
    halo_send, halo_recv, map_send, map_recv, vec_send, vec_recv,
):
    cells, groups, nv, nz = res.shape
    gx = lax.axis_index("gx")
    yz = lax.axis_index("yz")
    has_low = yz > 0
    has_high = yz < n_yz - 1

    barrier = pltpu.get_barrier_semaphore()
    for k in range(1, n_gx):
        pl.semaphore_signal(
            barrier, inc=1, device_id=(lax.rem(gx + k, n_gx), yz), device_id_type=MESH
        )

    @pl.when(has_low)
    def _():
        pl.semaphore_signal(barrier, inc=1, device_id=(gx, yz - 1), device_id_type=MESH)

    @pl.when(has_high)
    def _():
        pl.semaphore_signal(barrier, inc=1, device_id=(gx, yz + 1), device_id_type=MESH)

    def combos(x, carry):
        first, second = res[x, 0], res[x, 1]
        snd[0, x] = first - 8.0 * second
        snd[1, x] = 8.0 * first - second
        return carry

    lax.fori_loop(0, cells, combos, 0)

    pl.semaphore_wait(
        barrier, n_gx - 1 + jnp.where(has_low, 1, 0) + jnp.where(has_high, 1, 0)
    )

    pieces = cells // chunk

    def halo(direction, g, c):
        part = pl.ds(c * chunk, chunk)
        if direction == 0:
            src = snd.at[0, part] if g == 0 else res.at[part, 1]
            dst, where = low, yz + 1
        else:
            src = res.at[part, 0] if g == 0 else snd.at[1, part]
            dst, where = high, yz - 1
        return pltpu.make_async_remote_copy(
            src_ref=src,
            dst_ref=dst.at[g, part],
            send_sem=halo_send.at[direction, g, c],
            recv_sem=halo_recv.at[direction, g, c],
            device_id=(gx, where),
            device_id_type=MESH,
        )

    @pl.when(has_high)
    def _():
        for g in range(groups):
            for c in range(pieces):
                halo(0, g, c).start()

    @pl.when(has_low)
    def _():
        for g in range(groups):
            for c in range(pieces):
                halo(1, g, c).start()

    @pl.when(jnp.logical_not(has_low))
    def _():
        low[...] = jnp.zeros_like(low)

    @pl.when(jnp.logical_not(has_high))
    def _():
        high[...] = jnp.zeros_like(high)

    for g in range(groups):
        kind = kinds[g]
        for n, block in enumerate((flux[kind] * (1.0 / 12.0), -up[kind], -down[kind])):
            table[g, n, 0], table[g, n, 1] = split(block.T)

    def held(g, n):
        return table[g, n, 0], table[g, n, 1]

    def put(ref, g, x, pair):
        ref[g, x, 0], ref[g, x, 1] = pair

    def get(ref, g, x):
        return ref[g, x, 0], ref[g, x, 1]

    def steps(x, carry):
        for g in range(groups):
            v = split(inv[x, g].T)
            put(vt, g, x, v)
            put(ft, g, x, split(mul(v, held(g, 1))))
            put(bt, g, x, split(mul(v, held(g, 2))))
        return carry

    lax.fori_loop(0, cells, steps, 0)

    row = lax.broadcasted_iota(jnp.int32, (nv, 2 * nv), 0)
    col = lax.broadcasted_iota(jnp.int32, (nv, 2 * nv), 1)
    first_unit = (row == col).astype(F32)
    second_unit = (row + nv == col).astype(F32)

    for g in range(groups):
        hom[g, 0] = first_unit

    def hom_forward(x, carry):
        for g in range(groups):
            hom[g, x + 1] = mul(get(ft, g, x), split(hom[g, x]))
        return carry

    lax.fori_loop(0, cells, hom_forward, 0)

    def hom_backward(i, state):
        x = cells - 1 - i
        new = []
        for g in range(groups):
            m = hom[g, x + 1] + mul(get(bt, g, x), split(state[g]))
            put(resp, g, x, split(m))
            new.append(m)
        return tuple(new)

    firsts = lax.fori_loop(0, cells, hom_backward, (second_unit,) * groups)
    for g in range(groups):
        gmap[gx, g, :nv] = hom[g, cells]
        gmap[gx, g, nv:] = firsts[g]

    def share_map(k):
        return pltpu.make_async_remote_copy(
            src_ref=gmap.at[gx],
            dst_ref=gmap.at[gx],
            send_sem=map_send.at[k],
            recv_sem=map_recv.at[gx],
            device_id=(lax.rem(gx + k, n_gx), yz),
            device_id_type=MESH,
        )

    def take_map(k):
        source = lax.rem(gx + k, n_gx)
        return pltpu.make_async_remote_copy(
            src_ref=gmap.at[source],
            dst_ref=gmap.at[source],
            send_sem=map_send.at[k],
            recv_sem=map_recv.at[source],
            device_id=(source, yz),
            device_id_type=MESH,
        )

    def share_vec(g, k):
        return pltpu.make_async_remote_copy(
            src_ref=gvec.at[g, gx],
            dst_ref=gvec.at[g, gx],
            send_sem=vec_send.at[g, k],
            recv_sem=vec_recv.at[g, gx],
            device_id=(lax.rem(gx + k, n_gx), yz),
            device_id_type=MESH,
        )

    def take_vec(g, k):
        source = lax.rem(gx + k, n_gx)
        return pltpu.make_async_remote_copy(
            src_ref=gvec.at[g, source],
            dst_ref=gvec.at[g, source],
            send_sem=vec_send.at[g, k],
            recv_sem=vec_recv.at[g, source],
            device_id=(source, yz),
            device_id_type=MESH,
        )

    for k in range(1, n_gx):
        share_map(k).start()

    for g in range(groups):
        c_state = jnp.zeros((nv, nz), F32)
        for c in range(pieces):
            @pl.when(has_low)
            def _():
                halo(0, g, c).wait_recv()

            @pl.when(has_high)
            def _():
                halo(1, g, c).wait_recv()

            def forward(x, state):
                if g == 0:
                    derivative = 8.0 * res[x, 1] + low[g, x] - high[g, x]
                else:
                    derivative = low[g, x] + high[g, x] - 8.0 * res[x, 0]
                kind = cat[x][g : g + 1]
                weight = jnp.where(kind == 0, 1.0, jnp.where(kind == 2, 0.5, 0.0))
                force = weight * (res[x, g] + mul(held(g, 0), split(derivative)))
                state = mul(get(vt, g, x), split(force)) + mul(get(ft, g, x), split(state))
                cs[g, x] = state
                return state

            c_state = lax.fori_loop(c * chunk, (c + 1) * chunk, forward, c_state)

        def backward(i, state):
            x = cells - 1 - i
            state = cs[g, x] + mul(get(bt, g, x), split(state))
            cs[g, x] = state
            return state

        l_state = lax.fori_loop(0, cells, backward, jnp.zeros((nv, nz), F32))
        gvec[g, gx, :nv] = c_state
        gvec[g, gx, nv:] = l_state
        for k in range(1, n_gx):
            share_vec(g, k).start()

    for k in range(1, n_gx):
        take_map(k).wait_recv()

    for g in range(groups):
        for k in range(1, n_gx):
            take_vec(g, k).wait_recv()

        def ahead(j, state):
            cin[g, j, :nv] = state
            return gvec[g, j, :nv] + mul(split(gmap[j, g, :nv, :nv]), split(state))

        lax.fori_loop(0, n_gx, ahead, jnp.zeros((nv, nz), F32))

        def behind(i, state):
            j = n_gx - 1 - i
            cin[g, j, nv:] = state
            return gvec[g, j, nv:] + mul(split(gmap[j, g, nv:]), split(cin[g, j]))

        def behind_step(i, state):
            return behind(i, state)

        lax.fori_loop(0, n_gx, behind_step, jnp.zeros((nv, nz), F32))
        into[g, 0], into[g, 1] = split(cin[g, gx])

        def finish(x, carry):
            out[x, g] = cs[g, x] + mul(get(resp, g, x), (into[g, 0], into[g, 1]))
            return carry

        lax.fori_loop(0, cells, finish, 0)

    @pl.when(has_high)
    def _():
        for g in range(groups):
            for c in range(pieces):
                halo(0, g, c).wait_send()

    @pl.when(has_low)
    def _():
        for g in range(groups):
            for c in range(pieces):
                halo(1, g, c).wait_send()

    for k in range(1, n_gx):
        share_map(k).wait_send()
        for g in range(groups):
            share_vec(g, k).wait_send()


def per_device(n_gx, n_yz, residual, inverses, upwind, downwind, flux_y, kinds, volume_category):
    cells, groups, nv, nz = residual.shape
    chunk = next(c for c in (3, 4, 2, 1) if cells % c == 0)
    pieces = cells // chunk
    vmem = pl.BlockSpec(memory_space=pltpu.VMEM)
    swept = pl.pallas_call(
        functools.partial(kernel, n_gx, n_yz, chunk),
        out_shape=jax.ShapeDtypeStruct(residual.shape, F32),
        in_specs=[pl.BlockSpec(memory_space=pltpu.SMEM)] + [vmem] * 6,
        out_specs=vmem,
        scratch_shapes=[
            pltpu.VMEM((2, cells, nv, nz), F32),
            pltpu.VMEM((groups, cells, nv, nz), F32),
            pltpu.VMEM((groups, cells, nv, nz), F32),
            pltpu.VMEM((groups, 3, 2, nv, nv), BF16),
            pltpu.VMEM((groups, cells, 2, nv, nv), BF16),
            pltpu.VMEM((groups, cells, 2, nv, nv), BF16),
            pltpu.VMEM((groups, cells, 2, nv, nv), BF16),
            pltpu.VMEM((groups, cells + 1, nv, 2 * nv), F32),
            pltpu.VMEM((groups, cells, 2, nv, 2 * nv), BF16),
            pltpu.VMEM((groups, cells, nv, nz), F32),
            pltpu.VMEM((n_gx, groups, 2 * nv, 2 * nv), F32),
            pltpu.VMEM((groups, n_gx, 2 * nv, nz), F32),
            pltpu.VMEM((groups, n_gx, 2 * nv, nz), F32),
            pltpu.VMEM((groups, 2, 2 * nv, nz), BF16),
            pltpu.SemaphoreType.DMA((2, groups, pieces)),
            pltpu.SemaphoreType.DMA((2, groups, pieces)),
            pltpu.SemaphoreType.DMA((n_gx,)),
            pltpu.SemaphoreType.DMA((n_gx,)),
            pltpu.SemaphoreType.DMA((groups, n_gx)),
            pltpu.SemaphoreType.DMA((groups, n_gx)),
        ],
        compiler_params=pltpu.CompilerParams(
            collective_id=0, has_side_effects=True, vmem_limit_bytes=48 * 1024 * 1024
        ),
    )(kinds, residual, inverses, upwind, downwind, flux_y, volume_category)
    return jnp.where((volume_category != 1)[:, :, None, :], swept, 0.0)


def solution(mesh):
    in_specs = (
        P("gx", "yz", None, None),
        P("gx", "yz", None, None),
        P(),
        P(),
        P(),
        P("yz"),
        P("gx", "yz", None),
    )
    out_specs = P("gx", "yz", None, None)
    return jax.shard_map(
        functools.partial(per_device, mesh.shape["gx"], mesh.shape["yz"]),
        mesh=mesh,
        in_specs=in_specs,
        out_specs=out_specs,
        check_vma=False,
    )
```

time: 90.9 us -> 48.4 us (0.53)
  Pallas kernels: 0 us -> 41.1 us
  blocking collectives: 40.8 us -> 0 us
  matrix products: 33.2 us -> 0 us
  starting transfers between devices: 6.84 us -> 0 us
  loops' own time: 2.41 us -> 0 us
    pallas_call x0 -> x1, Pallas kernels: none -> 41.1 us  [per_device(): pl.pallas_call(functools.partial(kernel, n_gx, n_yz, chunk), out_shape=ja...]
    all_gather x4 -> x0, blocking collectives: 40.8 us -> none  [carried_in(): gathered = jax.tree.map(lambda a: lax.all_gather(a, axis), part)]
    dot_general x133 -> x0, matrix products: 33.2 us -> none  [the longest x103 20.6 us: apply_transposed(): return jnp.einsum('gab,gaz->gbz', matrices, vectors, precision=HIGHEST)]
    ppermute x2 -> x0, starting transfers between devices: 6.84 us -> none  [the longest x1 5.56 us: extended(): lax.ppermute(lax.slice_in_dim(block, block.shape[dim] - width, None, axis...]
    another operation x8 -> x0, loops' own time: 2.41 us -> none  [the longest x2 0.73 us: backward_pass(): lax.scan(backward_step, entering_back, (eliminated, inverses), reverse=True)]
    unnamed x12 -> x14, local copies, waits for them, and re-layouts: 2.82 us -> 5.12 us
    reshape x3 -> x0, local copies, waits for them, and re-layouts: 1.3 us -> none  [select_rows(): table.reshape(kind_count, -1)]
    select_n x0 -> x1, other arithmetic: none -> 0.96 us  [per_device(): return jnp.where((volume_category != 1)[:, :, None, :], swept, 0.0)]
  transfers between devices with their start and end apart: 2 -> 0, of which waited for: 0 -> 0; matrix products, arithmetic and copies ran while one was open for 14% -> 0% of each run, Pallas kernels for 0% -> 0%
where the time goes in v1:
time: 48.4 us; the launch traced here: 48 us
  Pallas kernels  41.1 us (85%)
  local copies, waits for them, and re-layouts  5.12 us (11%)
  other arithmetic  1.74 us (4%)
    pallas_call x1, Pallas kernels, per_device(): pl.pallas_call(functools.partial(kernel, n_gx, n_yz, chunk), out_shape=ja...  41.1 us
    unnamed x14, local copies, waits for them, and re-layouts  5.12 us

profile of v1, /device:TPU:1, one launch (start us, length us, event | category | flops | bytes accessed | tf_op | source)
XLA Modules:
  0.0 48.0 jit_solution(3123246893725205128)
XLA Ops:
  0.0 0.0 copy-start.5
  0.0 0.0 copy-start.6
  0.0 0.8 %broadcast_compare_fusion = pred[12,2,128]{2,1,0:T(4,128)(4,1)S(1)} fusion(s32[12,2,128]{2,1,0:T(2,128)} %cat.1), kind=kLoop, calls=%fused_computation.1 | loop fusion | flops 3072 | bytes 15360 | tf_op jit(solution)/shard_map/ne | solution.py:322
  0.8 0.0 copy-done.5
  0.8 0.0 copy-done.6
  0.8 0.0 copy-start
  0.8 1.1 %copy-done = f32[12,2,64,128]{3,2,1,0:T(8,128)S(1)} copy-done((f32[12,2,64,128]{3,2,1,0:T(8,128)S(1)}, f32[12,2,64,128]{3,2,1,0:T(8,128)}, u32[]{:S(2)}) %copy-start) | copy-done | bytes 786456
  1.9 0.0 copy-start.1
  2.0 1.1 %copy-done.1 = f32[12,2,64,64]{3,2,1,0:T(8,128)S(1)} copy-done((f32[12,2,64,64]{3,2,1,0:T(8,128)S(1)}, f32[12,2,64,64]{3,2,1,0:T(8,128)}, u32[]{:S(2)}) %copy-start.1) | copy-done | bytes 393240
  3.1 0.0 copy-start.2
  3.1 0.9 %copy-done.2 = f32[8,64,64]{2,1,0:T(8,128)S(1)} copy-done((f32[8,64,64]{2,1,0:T(8,128)S(1)}, f32[8,64,64]{2,1,0:T(8,128)}, u32[]{:S(2)}) %copy-start.2) | copy-done | bytes 131096
  4.0 0.0 copy-start.3
  4.0 0.9 %copy-done.3 = f32[8,64,64]{2,1,0:T(8,128)S(1)} copy-done((f32[8,64,64]{2,1,0:T(8,128)S(1)}, f32[8,64,64]{2,1,0:T(8,128)}, u32[]{:S(2)}) %copy-start.3) | copy-done | bytes 131096
  5.0 0.0 copy-start.4
  5.0 0.9 %copy-done.4 = f32[8,64,64]{2,1,0:T(8,128)S(1)} copy-done((f32[8,64,64]{2,1,0:T(8,128)S(1)}, f32[8,64,64]{2,1,0:T(8,128)}, u32[]{:S(2)}) %copy-start.4) | copy-done | bytes 131096
  5.9 41.1 %shard_map.73 = f32[12,2,64,128]{3,2,1,0:T(8,128)S(1)} custom-call(s32[2]{0:T(128)S(1)} %copy-done.6, f32[12,2,64,128]{3,2,1,0:T(8,128)S(1)} %copy-done, f32[12,2,64,64]{3,2,1,0:T(8,128)S(1)} %copy-done.1, f32[8,64,64]{2,1,0:T(8,128)S(1)} %copy-done.2, f32[8,64,64]{2,1,0:T(8,128)S(1)} %copy-done.3, f32[8,64,64]{2,1,0:T(8,128)S(1)} %copy-done.4, ...), custom_call_target="tpu_custom_call" | custom-call | tf_op jit(solution)/shard_map/pallas_call | solution.py:291
  47.1 1.0 %broadcast_select_fusion = f32[12,2,64,128]{3,2,1,0:T(8,128)} fusion(f32[12,2,64,128]{3,2,1,0:T(8,128)S(1)} %shard_map.73, pred[12,2,128]{2,1,0:T(4,128)(4,1)S(1)} %broadcast_compare_fusion), kind=kLoop, calls=%fused_computation | loop fusion | flops 196608 | bytes 1575936 | tf_op jit(solution)/shard_map/jit(_where)/select_n | solution.py:322
Async XLA Ops:
  0.0 0.8 %copy-start.5 = (s32[12,2,128]{2,1,0:T(2,128)S(1)}, s32[12,2,128]{2,1,0:T(2,128)}, u32[]{:S(2)}) copy-start(s32[12,2,128]{2,1,0:T(2,128)} %cat.1) | copy-start | bytes 36868
  0.0 0.8 %copy-start.6 = (s32[2]{0:T(128)S(1)}, s32[2]{0:T(128)}, u32[]{:S(2)}) copy-start(s32[2]{0:T(128)} %kinds.1) | copy-start | bytes 28
  0.8 1.1 %copy-start = (f32[12,2,64,128]{3,2,1,0:T(8,128)S(1)}, f32[12,2,64,128]{3,2,1,0:T(8,128)}, u32[]{:S(2)}) copy-start(f32[12,2,64,128]{3,2,1,0:T(8,128)} %res.1) | copy-start | bytes 2359300
  1.9 1.1 %copy-start.1 = (f32[12,2,64,64]{3,2,1,0:T(8,128)S(1)}, f32[12,2,64,64]{3,2,1,0:T(8,128)}, u32[]{:S(2)}) copy-start(f32[12,2,64,64]{3,2,1,0:T(8,128)} %inv.1) | copy-start | bytes 1179652
  3.1 0.9 %copy-start.2 = (f32[8,64,64]{2,1,0:T(8,128)S(1)}, f32[8,64,64]{2,1,0:T(8,128)}, u32[]{:S(2)}) copy-start(f32[8,64,64]{2,1,0:T(8,128)} %up.1) | copy-start | bytes 393220
  4.0 0.9 %copy-start.3 = (f32[8,64,64]{2,1,0:T(8,128)S(1)}, f32[8,64,64]{2,1,0:T(8,128)}, u32[]{:S(2)}) copy-start(f32[8,64,64]{2,1,0:T(8,128)} %down.1) | copy-start | bytes 393220
  5.0 0.9 %copy-start.4 = (f32[8,64,64]{2,1,0:T(8,128)S(1)}, f32[8,64,64]{2,1,0:T(8,128)}, u32[]{:S(2)}) copy-start(f32[8,64,64]{2,1,0:T(8,128)} %flux.1) | copy-start | bytes 393220

commit v2 on v1

v2 whole, which is shorter than its diff:
```python
import functools

import jax
import jax.numpy as jnp
from jax import lax
from jax.experimental import pallas as pl
from jax.experimental.pallas import tpu as pltpu
from jax.sharding import PartitionSpec as P

MESH = pl.DeviceIdType.MESH
F32 = jnp.float32
BF16 = jnp.bfloat16


def split(a):
    high = a.astype(BF16)
    return high, (a - high.astype(F32)).astype(BF16)


def mul(a, b):
    ah, al = a
    bh, bl = b
    d = functools.partial(jnp.dot, preferred_element_type=F32)
    return d(ah, bh) + (d(ah, bl) + d(al, bh))


def loop(count, body, carry, unroll=1):
    unroll = unroll if count % unroll == 0 else 1

    def several(i, carry):
        for u in range(unroll):
            carry = body(i * unroll + u, carry)
        return carry

    return lax.fori_loop(0, count // unroll, several, carry)


def kernel(
    n_gx, n_yz, chunk, kinds, res_hbm, inv_hbm, up_hbm, down_hbm, flux_hbm, cat_hbm, out,
    res, inv, up, down, flux, cat,
    snd, low, high, table, vt, ft, bt, hom, omega, lam, resp, cs, gmap, gvec, wc, wl, into, side, wide_state, tall,
    load_sem, halo_send, halo_recv, map_send, map_recv, vec_send, vec_recv,
):
    cells, groups, nv, nz = res.shape
    half = n_gx // 2
    pieces = cells // chunk
    gx = lax.axis_index("gx")
    yz = lax.axis_index("yz")
    partner = gx + 1 - 2 * lax.rem(gx, 2)
    has_low = yz > 0
    has_high = yz < n_yz - 1

    loads = [
        pltpu.make_async_copy(source, target, load_sem.at[n])
        for n, (source, target) in enumerate(
            (
                (res_hbm, res), (inv_hbm, inv), (up_hbm, up), (down_hbm, down),
                (flux_hbm, flux), (cat_hbm, cat),
            )
        )
    ]
    for load in loads:
        load.start()

    def peer(k):
        return lax.rem(gx + 2 * k, n_gx)

    barrier = pltpu.get_barrier_semaphore()
    for k in range(1, half):
        pl.semaphore_signal(barrier, inc=1, device_id=(peer(k), yz), device_id_type=MESH)
    pl.semaphore_signal(barrier, inc=1, device_id=(partner, yz), device_id_type=MESH)

    @pl.when(has_low)
    def _():
        pl.semaphore_signal(barrier, inc=1, device_id=(gx, yz - 1), device_id_type=MESH)

    @pl.when(has_high)
    def _():
        pl.semaphore_signal(barrier, inc=1, device_id=(gx, yz + 1), device_id_type=MESH)

    pl.semaphore_wait(barrier, half + jnp.where(has_low, 1, 0) + jnp.where(has_high, 1, 0))

    def halo(direction, g, c):
        part = pl.ds(c * chunk, chunk)
        if direction == 0:
            src = snd.at[0, part] if g == 0 else res_hbm.at[part, 1]
            dst, where = low, yz + 1
        else:
            src = res_hbm.at[part, 0] if g == 0 else snd.at[1, part]
            dst, where = high, yz - 1
        return pltpu.make_async_remote_copy(
            src_ref=src,
            dst_ref=dst.at[g, part],
            send_sem=halo_send.at[direction, g, c],
            recv_sem=halo_recv.at[direction, g, c],
            device_id=(gx, where),
            device_id_type=MESH,
        )

    @pl.when(has_low)
    def _():
        for c in range(pieces):
            halo(1, 0, c).start()

    loads[0].wait()

    for c in range(pieces):
        for x in range(c * chunk, (c + 1) * chunk):
            snd[0, x] = res[x, 0] - 8.0 * res[x, 1]

        @pl.when(has_high)
        def _():
            halo(0, 0, c).start()

    @pl.when(has_high)
    def _():
        for c in range(pieces):
            halo(0, 1, c).start()

    for c in range(pieces):
        for x in range(c * chunk, (c + 1) * chunk):
            snd[1, x] = 8.0 * res[x, 0] - res[x, 1]

        @pl.when(has_low)
        def _():
            halo(1, 1, c).start()

    @pl.when(jnp.logical_not(has_low))
    def _():
        low[...] = jnp.zeros_like(low)

    @pl.when(jnp.logical_not(has_high))
    def _():
        high[...] = jnp.zeros_like(high)

    for load in loads[1:]:
        load.wait()

    for g in range(groups):
        kind = kinds[g]
        for n, block in enumerate((flux[kind] * (1.0 / 12.0), -up[kind], -down[kind])):
            table[g, n, 0], table[g, n, 1] = split(block.T)

    def held(g, n):
        return table[g, n, 0], table[g, n, 1]

    def put(ref, g, x, pair):
        ref[g, x, 0], ref[g, x, 1] = pair

    def get(ref, g, x):
        return ref[g, x, 0], ref[g, x, 1]

    def steps(x, carry):
        for g in range(groups):
            v = split(inv[x, g].T)
            put(vt, g, x, v)
            put(ft, g, x, split(mul(v, held(g, 1))))
            put(bt, g, x, split(mul(v, held(g, 2))))
        return carry

    loop(cells, steps, 0, 4)

    row = lax.broadcasted_iota(jnp.int32, (nv, 2 * nv), 0)
    col = lax.broadcasted_iota(jnp.int32, (nv, 2 * nv), 1)
    first_unit = (row == col).astype(F32)
    second_unit = (row + nv == col).astype(F32)
    square_row = lax.broadcasted_iota(jnp.int32, (nv, nv), 0)
    square_col = lax.broadcasted_iota(jnp.int32, (nv, nv), 1)
    unit = (square_row == square_col).astype(F32)
    for g in range(groups):
        hom[g, 0] = first_unit
        omega[g, 0] = unit

    def hom_forward(x, carry):
        for g in range(groups):
            hom[g, x + 1] = mul(get(ft, g, x), split(hom[g, x]))
            omega[g, x + 1] = mul(split(omega[g, x]), get(bt, g, x))
        return carry

    loop(cells, hom_forward, 0)

    for g in range(groups):
        side[g] = jnp.zeros((nv, nv), F32)
        wide_state[g] = second_unit

    def hom_backward(i, carry):
        x = cells - 1 - i
        for g in range(groups):
            m = hom[g, x + 1] + mul(get(bt, g, x), split(wide_state[g]))
            put(resp, g, x, split(m))
            wide_state[g] = m
            now = split(omega[g, x] + side[g])
            put(lam, g, x, now)
            side[g] = mul(now, get(ft, g, x))
        return carry

    loop(cells, hom_backward, 0)
    for g in range(groups):
        gmap[gx, g * nv : (g + 1) * nv] = wide_state[g]
    gmap[gx, groups * nv :] = jnp.concatenate(
        [hom[g, cells][:, :nv] for g in range(groups)], axis=1
    )

    def share(buffer, send, recv, slot, target, k):
        return pltpu.make_async_remote_copy(
            src_ref=buffer.at[slot],
            dst_ref=buffer.at[slot],
            send_sem=send.at[k],
            recv_sem=recv.at[slot],
            device_id=(target, yz),
            device_id_type=MESH,
        )

    def offer(*where):
        for k in range(1, half):
            share(*where, gx, peer(k), k).start()
        share(*where, gx, partner, 0).start()

    def relay(*where):
        for k in range(1, half):
            share(*where, peer(k), peer(k), k).wait_recv()
            share(*where, peer(k), partner, half + k).start()

    def collect(*where):
        share(*where, partner, partner, 0).wait_recv()
        for k in range(1, half):
            share(*where, lax.rem(partner + 2 * k, n_gx), partner, half + k).wait_recv()

    def release(*where):
        share(*where, gx, partner, 0).wait_send()
        for k in range(1, half):
            share(*where, gx, peer(k), k).wait_send()
            share(*where, peer(k), partner, half + k).wait_send()

    maps = (gmap, map_send, map_recv)
    vecs = [(gvec.at[g], vec_send.at[g], vec_recv.at[g]) for g in range(groups)]
    offer(*maps)

    def local_forward(g):
        state = (jnp.zeros((nv, nz), F32), jnp.zeros((nv, nz), F32))
        for c in range(pieces):
            @pl.when(has_low)
            def _():
                halo(0, g, c).wait_recv()

            @pl.when(has_high)
            def _():
                halo(1, g, c).wait_recv()

            def forward(i, state):
                x = c * chunk + i
                last, first = state
                if g == 0:
                    derivative = 8.0 * res[x, 1] + low[g, x] - high[g, x]
                else:
                    derivative = low[g, x] + high[g, x] - 8.0 * res[x, 0]
                kind = cat[x][g : g + 1]
                weight = jnp.where(kind == 0, 1.0, jnp.where(kind == 2, 0.5, 0.0))
                force = weight * (res[x, g] + mul(held(g, 0), split(derivative)))
                driven = mul(get(vt, g, x), split(force))
                last = driven + mul(get(ft, g, x), split(last))
                first = first + mul(get(lam, g, x), split(driven))
                cs[g, x] = last
                return last, first

            state = loop(chunk, forward, state, chunk)
        gvec[g, gx, :nv] = state[0]
        gvec[g, gx, nv:] = state[1]

    def local_backward(g):
        def backward(i, state):
            x = cells - 1 - i
            state = cs[g, x] + mul(get(bt, g, x), split(state))
            cs[g, x] = state
            return state

        loop(cells, backward, jnp.zeros((nv, nz), F32))

    def finish(g):
        total = jnp.zeros((2 * nv, nz), F32)
        tail = jnp.zeros((nv, nz), F32)
        for j in range(n_gx):
            total = total + mul(get(wc, g, j), split(gvec[g, j, :nv]))
            tail = tail + mul(get(wl, g, j), split(gvec[g, j, nv:]))
        into[g, 0, :nv], into[g, 1, :nv] = split(total[:nv])
        into[g, 0, nv:], into[g, 1, nv:] = split(total[nv:] + tail)

        def fix(x, carry):
            value = cs[g, x] + mul(get(resp, g, x), (into[g, 0], into[g, 1]))
            out[x, g] = jnp.where(cat[x][g : g + 1] != 1, value, 0.0)
            return carry

        loop(cells, fix, 0, 4)

    local_forward(0)
    offer(*vecs[0])
    relay(*maps)
    local_backward(0)
    collect(*maps)

    for g in range(groups):
        side[g] = jnp.zeros((nv, nv), F32)
        tall[g] = jnp.zeros((2 * nv, nv), F32)

    def suffix(j, carry):
        here = jnp.where(gx == j, 1.0, 0.0)
        for g in range(groups):
            e = split(side[g])
            put(wl, g, j, e)
            both = mul(e, split(gmap[j, g * nv : (g + 1) * nv]))
            side[g] = both[:, nv:] + here * unit
            hom[g, j] = both
        return carry

    loop(n_gx, suffix, 0)

    def prefix(i, carry):
        j = n_gx - 1 - i
        here = jnp.where(gx == j, 1.0, 0.0)
        maps_here = gmap[j, groups * nv :]
        for g in range(groups):
            xs = split(tall[g])
            put(wc, g, j, xs)
            nxt = mul(xs, split(maps_here[:, g * nv : (g + 1) * nv]))
            tall[g, :nv] = nxt[:nv] + here * unit
            tall[g, nv:] = nxt[nv:] + hom[g, j][:, :nv]
        return carry

    loop(n_gx, prefix, 0)

    relay(*vecs[0])
    for g in range(1, groups):
        local_forward(g)
        offer(*vecs[g])
        local_backward(g)
        relay(*vecs[g])
    for g in range(groups):
        collect(*vecs[g])
        finish(g)

    @pl.when(has_high)
    def _():
        for g in range(groups):
            for c in range(pieces):
                halo(0, g, c).wait_send()

    @pl.when(has_low)
    def _():
        for g in range(groups):
            for c in range(pieces):
                halo(1, g, c).wait_send()

    release(*maps)
    for g in range(groups):
        release(*vecs[g])


def per_device(n_gx, n_yz, residual, inverses, upwind, downwind, flux_y, kinds, volume_category):
    cells, groups, nv, nz = residual.shape
    chunk = next(c for c in (3, 4, 2, 1) if cells % c == 0)
    pieces = cells // chunk
    hbm = pl.BlockSpec(memory_space=pltpu.HBM)
    operands = (residual, inverses, upwind, downwind, flux_y, volume_category)
    square = pltpu.VMEM((groups, cells, 2, nv, nv), BF16)
    wide = pltpu.VMEM((groups, cells, nv, nz), F32)
    return pl.pallas_call(
        functools.partial(kernel, n_gx, n_yz, chunk),
        out_shape=jax.ShapeDtypeStruct(residual.shape, F32),
        in_specs=[pl.BlockSpec(memory_space=pltpu.SMEM)] + [hbm] * 6,
        out_specs=pl.BlockSpec(memory_space=pltpu.VMEM),
        scratch_shapes=[pltpu.VMEM(a.shape, a.dtype) for a in operands]
        + [
            pltpu.VMEM((2, cells, nv, nz), F32),
            wide,
            wide,
            pltpu.VMEM((groups, 3, 2, nv, nv), BF16),
            square,
            square,
            square,
            pltpu.VMEM((groups, max(cells, n_gx) + 1, nv, 2 * nv), F32),
            pltpu.VMEM((groups, cells + 1, nv, nv), F32),
            square,
            pltpu.VMEM((groups, cells, 2, nv, 2 * nv), BF16),
            wide,
            pltpu.VMEM((n_gx, (groups + 1) * nv, 2 * nv), F32),
            pltpu.VMEM((groups, n_gx, 2 * nv, nz), F32),
            pltpu.VMEM((groups, n_gx, 2, 2 * nv, nv), BF16),
            pltpu.VMEM((groups, n_gx, 2, nv, nv), BF16),
            pltpu.VMEM((groups, 2, 2 * nv, nz), BF16),
            pltpu.VMEM((groups, nv, nv), F32),
            pltpu.VMEM((groups, nv, 2 * nv), F32),
            pltpu.VMEM((groups, 2 * nv, nv), F32),
            pltpu.SemaphoreType.DMA((6,)),
            pltpu.SemaphoreType.DMA((2, groups, pieces)),
            pltpu.SemaphoreType.DMA((2, groups, pieces)),
            pltpu.SemaphoreType.DMA((n_gx,)),
            pltpu.SemaphoreType.DMA((n_gx,)),
            pltpu.SemaphoreType.DMA((groups, n_gx)),
            pltpu.SemaphoreType.DMA((groups, n_gx)),
        ],
        compiler_params=pltpu.CompilerParams(
            collective_id=0, has_side_effects=True, vmem_limit_bytes=67043328
        ),
    )(kinds, *operands)


def solution(mesh):
    in_specs = (
        P("gx", "yz", None, None),
        P("gx", "yz", None, None),
        P(),
        P(),
        P(),
        P("yz"),
        P("gx", "yz", None),
    )
    out_specs = P("gx", "yz", None, None)
    return jax.shard_map(
        functools.partial(per_device, mesh.shape["gx"], mesh.shape["yz"]),
        mesh=mesh,
        in_specs=in_specs,
        out_specs=out_specs,
        check_vma=False,
    )
```

time: 48.4 us -> 36.5 us (0.75)
  Pallas kernels: 41.1 us -> 33.8 us
  local copies, waits for them, and re-layouts: 5.12 us -> 2.09 us
  other arithmetic: 1.74 us -> 0 us
    pallas_call x1, Pallas kernels: 41.1 us -> 33.8 us  [per_device(): pl.pallas_call(functools.partial(kernel, n_gx, n_yz, chunk), out_shape=ja...]
    unnamed x14 -> x1, local copies, waits for them, and re-layouts: 5.12 us -> 2.09 us
    select_n x1 -> x0, other arithmetic: 0.96 us -> none  [per_device(): return jnp.where((volume_category != 1)[:, :, None, :], swept, 0.0)]
    ne x1 -> x0, other arithmetic: 0.79 us -> none  [per_device(): return jnp.where((volume_category != 1)[:, :, None, :], swept, 0.0)]
where the time goes in v2:
time: 36.5 us; the launch traced here: 35.9 us
  Pallas kernels  33.8 us (93%)
  local copies, waits for them, and re-layouts  2.09 us (6%)
    pallas_call x1, Pallas kernels, per_device(): pl.pallas_call(functools.partial(kernel, n_gx, n_yz, chunk), out_shape=ja...  33.8 us
    unnamed x1, local copies, waits for them, and re-layouts  2.09 us

profile of v2, /device:TPU:1, one launch (start us, length us, event | category | flops | bytes accessed | tf_op | source)
XLA Modules:
  0.0 35.9 jit_solution(2313427418739098479)
XLA Ops:
  0.0 33.8 %shard_map.73 = f32[12,2,64,128]{3,2,1,0:T(8,128)} custom-call(s32[2]{0:T(128)} %kinds.1, f32[12,2,64,128]{3,2,1,0:T(8,128)} %res_hbm.1, f32[12,2,64,64]{3,2,1,0:T(8,128)} %inv_hbm.1, f32[8,64,64]{2,1,0:T(8,128)} %up_hbm.1, f32[8,64,64]{2,1,0:T(8,128)} %down_hbm.1, f32[8,64,64]{2,1,0:T(8,128)} %flux_hbm.1, s32[12,2,128]{2,1,0:T(2,128)} %cat_hbm.1), custom_call_target="tpu_custom_call" | custom-call | tf_op jit(solution)/shard_map/pallas_call | solution.py:366
  33.9 2.1 %copy.9 = f32[12,2,64,128]{3,2,1,0:T(8,128)} copy(f32[12,2,64,128]{3,2,1,0:T(8,128)} %shard_map.73) | data formatting | bytes 1572864

commit v3 on v2

--- a/solution.py
+++ b/solution.py
@@ -36,9 +36,9 @@
 
 
 def kernel(
-    n_gx, n_yz, chunk, kinds, res_hbm, inv_hbm, up_hbm, down_hbm, flux_hbm, cat_hbm, out,
-    res, inv, up, down, flux, cat,
-    snd, low, high, table, vt, ft, bt, hom, omega, lam, resp, cs, gmap, gvec, wc, wl, into, side, wide_state, tall,
+    n_gx, n_yz, chunk, res_hbm, inv_hbm, up_hbm, down_hbm, flux_hbm, cat_hbm, kinds_hbm, out,
+    res, inv, up, down, flux, cat, kinds,
+    snd, low, high, table, vt, ft, bt, hom, omega, lam, resp, cs, gmap, gvec, wc, wl, into, side, wide_state, tall, into_state,
     load_sem, halo_send, halo_recv, map_send, map_recv, vec_send, vec_recv,
 ):
     cells, groups, nv, nz = res.shape
@@ -55,7 +55,7 @@
         for n, (source, target) in enumerate(
             (
                 (res_hbm, res), (inv_hbm, inv), (up_hbm, up), (down_hbm, down),
-                (flux_hbm, flux), (cat_hbm, cat),
+                (flux_hbm, flux), (cat_hbm, cat), (kinds_hbm, kinds),
             )
         )
     ]
@@ -267,14 +267,19 @@
         gvec[g, gx, :nv] = state[0]
         gvec[g, gx, nv:] = state[1]
 
-    def local_backward(g):
-        def backward(i, state):
-            x = cells - 1 - i
-            state = cs[g, x] + mul(get(bt, g, x), split(state))
-            cs[g, x] = state
-            return state
-
-        loop(cells, backward, jnp.zeros((nv, nz), F32))
+    def local_backward():
+        for g in range(groups):
+            into_state[g] = cs[g, cells - 1]
+
+        def backward(i, carry):
+            x = cells - 2 - i
+            for g in range(groups):
+                state = cs[g, x] + mul(get(bt, g, x), split(into_state[g]))
+                into_state[g] = state
+                cs[g, x] = state
+            return carry
+
+        lax.fori_loop(0, cells - 1, backward, 0)
 
     def finish(g):
         total = jnp.zeros((2 * nv, nz), F32)
@@ -295,7 +300,6 @@
     local_forward(0)
     offer(*vecs[0])
     relay(*maps)
-    local_backward(0)
     collect(*maps)
 
     for g in range(groups):
@@ -332,7 +336,8 @@
     for g in range(1, groups):
         local_forward(g)
         offer(*vecs[g])
-        local_backward(g)
+    local_backward()
+    for g in range(1, groups):
         relay(*vecs[g])
     for g in range(groups):
         collect(*vecs[g])
@@ -360,16 +365,17 @@
     chunk = next(c for c in (3, 4, 2, 1) if cells % c == 0)
     pieces = cells // chunk
     hbm = pl.BlockSpec(memory_space=pltpu.HBM)
-    operands = (residual, inverses, upwind, downwind, flux_y, volume_category)
+    operands = (residual, inverses, upwind, downwind, flux_y, volume_category, kinds)
     square = pltpu.VMEM((groups, cells, 2, nv, nv), BF16)
     wide = pltpu.VMEM((groups, cells, nv, nz), F32)
     return pl.pallas_call(
         functools.partial(kernel, n_gx, n_yz, chunk),
         out_shape=jax.ShapeDtypeStruct(residual.shape, F32),
-        in_specs=[pl.BlockSpec(memory_space=pltpu.SMEM)] + [hbm] * 6,
+        in_specs=[hbm] * 7,
         out_specs=pl.BlockSpec(memory_space=pltpu.VMEM),
-        scratch_shapes=[pltpu.VMEM(a.shape, a.dtype) for a in operands]
+        scratch_shapes=[pltpu.VMEM(a.shape, a.dtype) for a in operands[:-1]]
         + [
+            pltpu.SMEM(kinds.shape, kinds.dtype),
             pltpu.VMEM((2, cells, nv, nz), F32),
             wide,
             wide,
@@ -390,7 +396,8 @@
             pltpu.VMEM((groups, nv, nv), F32),
             pltpu.VMEM((groups, nv, 2 * nv), F32),
             pltpu.VMEM((groups, 2 * nv, nv), F32),
-            pltpu.SemaphoreType.DMA((6,)),
+            pltpu.VMEM((groups, nv, nz), F32),
+            pltpu.SemaphoreType.DMA((7,)),
             pltpu.SemaphoreType.DMA((2, groups, pieces)),
             pltpu.SemaphoreType.DMA((2, groups, pieces)),
             pltpu.SemaphoreType.DMA((n_gx,)),
@@ -399,9 +406,9 @@
             pltpu.SemaphoreType.DMA((groups, n_gx)),
         ],
         compiler_params=pltpu.CompilerParams(
-            collective_id=0, has_side_effects=True, vmem_limit_bytes=67043328
+            collective_id=0, has_side_effects=True, vmem_limit_bytes=48 * 1024 * 1024
         ),
-    )(kinds, *operands)
+    )(*(pltpu.with_memory_space_constraint(a, pltpu.HBM) for a in operands))
 
 
 def solution(mesh):

time: 36.5 us -> 32.7 us (0.90)
  Pallas kernels: 33.8 us -> 31.5 us
  local copies, waits for them, and re-layouts: 2.09 us -> 0.88 us
    pallas_call x1, Pallas kernels: 33.8 us -> 31.5 us  [per_device(): pl.pallas_call(functools.partial(kernel, n_gx, n_yz, chunk), out_shape=ja...]
    unnamed x1, local copies, waits for them, and re-layouts: 2.09 us -> 0.88 us
where the time goes in v3:
time: 32.7 us; the launch traced here: 32.4 us
  Pallas kernels  31.5 us (96%)
  local copies, waits for them, and re-layouts  0.88 us (3%)
    pallas_call x1, Pallas kernels, per_device(): pl.pallas_call(functools.partial(kernel, n_gx, n_yz, chunk), out_shape=ja...  31.5 us
    unnamed x1, local copies, waits for them, and re-layouts  0.88 us

profile of v3, /device:TPU:1, one launch (start us, length us, event | category | flops | bytes accessed | tf_op | source)
XLA Modules:
  0.0 32.4 jit_solution(17313577669191444048)
XLA Ops:
  0.0 31.5 %shard_map.73 = f32[12,2,64,128]{3,2,1,0:T(8,128)S(1)} custom-call(f32[12,2,64,128]{3,2,1,0:T(8,128)} %res_hbm.1, f32[12,2,64,64]{3,2,1,0:T(8,128)} %inv_hbm.1, f32[8,64,64]{2,1,0:T(8,128)} %up_hbm.1, f32[8,64,64]{2,1,0:T(8,128)} %down_hbm.1, f32[8,64,64]{2,1,0:T(8,128)} %flux_hbm.1, s32[12,2,128]{2,1,0:T(2,128)} %cat_hbm.1, s32[2]{0:T(128)} %kinds_hbm.1), custom_call_target="tpu_custom_call" | custom-call | tf_op jit(solution)/shard_map/pallas_call | solution.py:371
  31.5 0.9 %copy.9 = f32[12,2,64,128]{3,2,1,0:T(8,128)} copy(f32[12,2,64,128]{3,2,1,0:T(8,128)S(1)} %shard_map.73) | data formatting | bytes 1572864
